TPU v7x, 256 devices: a whole 4x4x8 slice. The times are simulated.
256 devices in a mesh: ex: 32 (over x, z), feat: 8 (over y, core).
Axes of the slice: x: 4, y: 4, z: 8, core: 2. Of those that a mesh axis runs over, the one named last changes fastest.
Arguments:
- train_grads: bfloat16 [16384, 32768], P('ex', 'feat'), may hold values from -0.03125 to 0.03125
- audit_grads: bfloat16 [2, 32, 32, 32768], P(None, 'ex', None, 'feat'), may hold values from -6 to 6
- owner_map: int32 [64], replicated, may hold values from 0 to 63, as said below
- pair_blocks: int32 [32, 32], P('ex'), may hold values from 0 to 63, as said below
- pair_counts: int32 [32], P('ex'), may hold values from 1 to 32, as said below
Outputs:
- tiles: float32 [32, 32, 32, 512], P('ex', 'feat')
Inputs may be any that keep to these rules, and one draw needn't show every extreme that they name: `owner_map`: a permutation of the audit blocks. `pair_blocks`: the 32 entries of each training block name audit blocks whose stored blocks lie on 32 different indices of ex (owner_map[a] % 32 differs); entries at or after pair_counts are not live. `pair_counts`: some training block has all 32 pairs live.
All inputs are finite; a program needn't handle non-finite values.
Results may differ from a plain program's by a relative error of at most 0.0003.
Values may be sent and summed in bfloat16 or wider, within the bound.
A program may use at most 64 MiB of HBM per device.

v0:
```python
import jax
import jax.numpy as jnp
from jax import lax
from jax.sharding import PartitionSpec as P


def shards(train_grads, audit_grads, owner_map, pair_blocks, pair_counts):
    peers = lax.axis_size("ex")
    stored = jnp.take(owner_map, pair_blocks[0])
    holder = stored % peers
    local = stored // peers
    order = jnp.arange(peers, dtype=jnp.int32)
    live = (order < pair_counts[0]).astype(jnp.float32)
    stored_count = audit_grads.shape[0]
    piece = lax.all_gather(audit_grads, "ex", axis=1, tiled=True)
    count = piece.shape[1]
    scores = jnp.einsum("jnaf,tf->jnat", piece, train_grads, preferred_element_type=jnp.float32)
    span = jnp.arange(count, dtype=jnp.int32)
    kinds = jnp.arange(stored_count, dtype=jnp.int32)
    pick = (
        (local[:, None, None] == kinds[None, :, None])
        & (holder[:, None, None] == span[None, None, :])
    ).astype(jnp.float32)
    summed = jnp.einsum("kjn,jnat->kat", pick, scores, precision=lax.Precision.HIGHEST)
    tiles = lax.psum_scatter(summed * live[:, None, None], "feat", scatter_dimension=0, tiled=True)
    return tiles[None]


def solution(mesh):
    in_specs = (P("ex", "feat"), P(None, "ex", None, "feat"), P(), P("ex", None), P("ex"))
    out_specs = P("ex", "feat", None, None)
    return jax.shard_map(shards, mesh=mesh, in_specs=in_specs, out_specs=out_specs, check_vma=False)
```

profile of v0, /device:TPU:2, one launch (start us, length us, event | category | flops | bytes accessed | tf_op | source)
XLA Modules:
  0.0 212.7 jit_solution(17355145147538234622)
XLA Ops:
  6.5 0.0 copy-start
  6.5 0.0 all-gather.2.cloned.1.call-start
  6.5 0.7 all-gather.2.cloned.1.call-update
  7.3 0.0 reduce-scatter.2.cloned.1.call-start
  8.0 0.7 fusion.10
  8.6 0.0 copy-done
  8.6 0.7 gather_fusion
  9.3 0.7 and_select_fusion.1
  10.0 0.1 iota_compare_fusion
  10.1 141.2 %all-gather.2.cloned.1.call-done = bf16[2,32,32,4096]{3,2,1,0:T(8,128)(2,1)} async-done(((bf16[2,1,32,4096]{3,2,1,0:T(8,128)(2,1)}), bf16[2,32,32,4096]{3,2,1,0:T(8,128)(2,1)}) %all-gather.2.cloned.1.call-update) | async-done | bytes 16777232 | tf_op jit(solution)/shard_map/all_gather | solution.py:15
  151.3 13.0 %fusion = f32[2,32,32,512]{3,2,1,0:T(8,128)S(1)} fusion(bf16[2,32,32,4096]{3,2,1,0:T(8,128)(2,1)} %all-gather.2.cloned.1.call-done, bf16[512,4096]{1,0:T(8,128)(2,1)} %param.5), kind=kOutput, calls=%fused_computation.1 | convolution fusion | flops 8589934592 | bytes 25165824 | tf_op jit(solution)/shard_map/jnaf,tf->jnat/dot_general | solution.py:17
  164.3 4.1 %bitcast_multiply_fusion = f32[32,32,512]{2,0,1:T(8,128)S(1)} fusion(f32[2,32,32,512]{3,2,1,0:T(8,128)S(1)} %fusion, f32[32]{0:T(128)S(1)} %compare_convert_fusion, pred[32,32]{1,0:T(8,128)(4,1)S(1)} %iota_compare_fusion, pred[32,2]{0,1:T(4,128)(4,1)S(1)} %iota_compare_fusion.1), kind=kOutput, calls=%fused_computation.5 | convolution fusion | flops 403179520 | bytes 6292672 | tf_op jit(solution)/shard_map/kjn,jnat->kat/dot_general | solution.py:24
  168.4 2.6 %copy.9 = f32[32,32,512]{2,1,0:T(8,128)} copy(f32[32,32,512]{2,0,1:T(8,128)S(1)} %bitcast_multiply_fusion) | data formatting | bytes 4194304 | tf_op jit(solution)/shard_map/mul | solution.py:25
  171.0 0.0 reduce-scatter.2.cloned.1.call-update
  171.0 34.9 %reduce-scatter.2.cloned.1.call-done = f32[4,32,512]{2,1,0:T(8,128)} async-done(((f32[32,32,512]{2,1,0:T(8,128)}), f32[4,32,512]{2,1,0:T(8,128)}) %reduce-scatter.2.cloned.1.call-update) | async-done | bytes 262160 | tf_op jit(solution)/shard_map/reduce_scatter | solution.py:25
  (4 shorter events, 0.0 us)
Async XLA Ops:
  6.5 2.1 copy-start
  6.5 144.8 %all-gather.2.cloned.1.call-start = ((), (), s32[]{:S(2)}) async-start(), calls=%async_computation.1 | async-start | bytes 17301504 | tf_op jit(solution)/shard_map/all_gather | solution.py:15
  7.3 198.6 %reduce-scatter.2.cloned.1.call-start = ((), (), s32[]{:S(2)}) async-start(), calls=%async_computation.2 | async-start | bytes 2359296 | tf_op jit(solution)/shard_map/reduce_scatter | solution.py:25
Sparse Core Ops, SparseCore 0:
  9.9 141.3 all-gather.1
  171.1 34.7 reduce-scatter.1
where the time goes:
time: 213 us
  waiting for transfers between devices  177 us (83%)
  matrix products  17.1 us (8%)
  between operations  14.1 us (7%)
  local copies, waits for them, and re-layouts  3.26 us (2%)
    all_gather x1, waiting for transfers between devices, shards(): piece = lax.all_gather(audit_grads, 'ex', axis=1, tiled=True)  141 us
    reduce_scatter x1, waiting for transfers between devices, shards(): lax.psum_scatter(summed * live[:, None, None], 'feat', scatter_dimension=...  34.9 us
    dot_general x1, matrix products, shards(): jnp.einsum('jnaf,tf->jnat', piece, train_grads, preferred_element_type=jn...  13 us
  transfers between devices with their start and end apart: 2, of which 2 were waited for; matrix products, arithmetic and copies ran while one was open for 1% of the time, Pallas kernels for 0%

commit v1 on v0

--- a/solution.py
+++ b/solution.py
@@ -12,7 +12,9 @@
     order = jnp.arange(peers, dtype=jnp.int32)
     live = (order < pair_counts[0]).astype(jnp.float32)
     stored_count = audit_grads.shape[0]
-    piece = lax.all_gather(audit_grads, "ex", axis=1, tiled=True)
+    piece = jnp.concatenate(
+        lax.all_to_all(jnp.stack([audit_grads] * lax.axis_size("ex")), "ex", 0, 0), axis=1
+    )
     count = piece.shape[1]
     scores = jnp.einsum("jnaf,tf->jnat", piece, train_grads, preferred_element_type=jnp.float32)
     span = jnp.arange(count, dtype=jnp.int32)

time: 213 us -> 499 us (2.34)
  waiting for transfers between devices: 177 us -> 446 us
  starting transfers between devices: 0.04 us -> 11.8 us
  local copies, waits for them, and re-layouts: 3.26 us -> 10 us
    all_to_all x0 -> x1, waiting for transfers between devices: none -> 408 us  [shards(): lax.all_to_all(jnp.stack([audit_grads] * lax.axis_size('ex')), 'ex', 0, 0)]
    all_gather x1 -> x0, waiting for transfers between devices: 141 us -> none  [shards(): piece = lax.all_gather(audit_grads, 'ex', axis=1, tiled=True)]
    all_to_all x0 -> x1, starting transfers between devices: none -> 11.8 us  [shards(): lax.all_to_all(jnp.stack([audit_grads] * lax.axis_size('ex')), 'ex', 0, 0)]
    another operation x0 -> x1, local copies, waits for them, and re-layouts: none -> 6.74 us  [shards(): jnp.stack([audit_grads] * lax.axis_size('ex'))]
  transfers between devices with their start and end apart: 2 -> 2, of which waited for: 2 -> 2; matrix products, arithmetic and copies ran while one was open for 1% -> 0% of each run, Pallas kernels for 0% -> 0%
where the time goes in v1:
time: 499 us
  waiting for transfers between devices  446 us (89%)
  matrix products  17.1 us (3%)
  between operations  14.1 us (3%)
  starting transfers between devices  11.8 us (2%)
  local copies, waits for them, and re-layouts  10 us (2%)
    all_to_all x1, waiting for transfers between devices, shards(): lax.all_to_all(jnp.stack([audit_grads] * lax.axis_size('ex')), 'ex', 0, 0)  408 us
    reduce_scatter x1, waiting for transfers between devices, shards(): lax.psum_scatter(summed * live[:, None, None], 'feat', scatter_dimension=...  38.3 us
    dot_general x1, matrix products, shards(): jnp.einsum('jnaf,tf->jnat', piece, train_grads, preferred_element_type=jn...  13 us
    all_to_all x1, starting transfers between devices, shards(): lax.all_to_all(jnp.stack([audit_grads] * lax.axis_size('ex')), 'ex', 0, 0)  11.8 us
  transfers between devices with their start and end apart: 2, of which 2 were waited for; matrix products, arithmetic and copies ran while one was open for 0% of the time, Pallas kernels for 0%

profile of v1, /device:TPU:2, one launch (start us, length us, event | category | flops | bytes accessed | tf_op | source)
XLA Modules:
  0.0 499.1 jit_solution(15050060060410629618)
XLA Ops:
  6.5 0.0 copy-start
  6.5 6.7 %stack.2 = bf16[32,2,1,32,4096]{4,3,1,2,0:T(8,128)(2,1)} broadcast(bf16[2,32,4096]{2,1,0:T(8,128)(2,1)} %bitcast.27), dimensions={1,3,4} | broadcast | bytes 17301504 | tf_op jit(solution)/shard_map/stack | solution.py:16
  13.3 0.0 copy-start.1
  13.3 11.8 %all-to-all-start = ((bf16[32,2,1,32,4096]{4,3,1,2,0:T(8,128)(2,1)}), bf16[32,2,1,32,4096]{4,3,1,2,0:T(8,128)(2,1)}, u32[]{:S(2)}, u32[]{:S(2)}) async-start(bf16[32,2,1,32,4096]{4,3,1,2,0:T(8,128)(2,1)} %stack.2), calls=%async_computation | async-start | bytes 33554432 | tf_op jit(solution)/shard_map/all_to_all | solution.py:16
  25.1 0.0 reduce-scatter.2.cloned.1.call-start
  25.8 0.0 copy-done.1
  25.8 0.0 copy-done
  25.8 0.7 gather_fusion
  26.6 0.1 iota_compare_fusion
  26.7 407.7 %all-to-all-done = bf16[32,2,1,32,4096]{4,3,1,2,0:T(8,128)(2,1)} async-done(((bf16[32,2,1,32,4096]{4,3,1,2,0:T(8,128)(2,1)}), bf16[32,2,1,32,4096]{4,3,1,2,0:T(8,128)(2,1)}, u32[]{:S(2)}, u32[]{:S(2)}) %all-to-all-start) | async-done | bytes 16777248 | tf_op jit(solution)/shard_map/all_to_all | solution.py:16
  434.3 13.0 %fusion = f32[2,32,32,512]{3,2,1,0:T(8,128)S(1)} fusion(bf16[32,2,1,32,4096]{4,3,1,2,0:T(8,128)(2,1)} %all-to-all-done, bf16[512,4096]{1,0:T(8,128)(2,1)} %param.5), kind=kOutput, calls=%fused_computation.1 | convolution fusion | flops 8589934592 | bytes 25165824 | tf_op jit(solution)/shard_map/jnaf,tf->jnat/dot_general | solution.py:19
  447.3 4.1 bitcast_multiply_fusion
  451.4 2.6 copy.12
  454.0 0.0 reduce-scatter.2.cloned.1.call-update
  454.0 38.3 %reduce-scatter.2.cloned.1.call-done = f32[4,32,512]{2,1,0:T(8,128)} async-done(((f32[32,32,512]{2,1,0:T(8,128)}), f32[4,32,512]{2,1,0:T(8,128)}) %reduce-scatter.2.cloned.1.call-update) | async-done | bytes 262160 | tf_op jit(solution)/shard_map/reduce_scatter | solution.py:27
  (6 shorter events, 0.0 us)
Async XLA Ops:
  6.5 19.3 %copy-start = (s32[64]{0:T(128)S(1)}, s32[64]{0:T(128)}, u32[]{:S(2)}) copy-start(s32[64]{0:T(128)} %param.7) | copy-start | bytes 772
  13.3 12.5 %copy-start.1 = (s32[1,32]{1,0:T(1,128)S(1)}, s32[1,32]{1,0:T(1,128)}, u32[]{:S(2)}) copy-start(s32[1,32]{1,0:T(1,128)} %param.8) | copy-start | bytes 388
  13.3 421.0 %all-to-all-start = ((bf16[32,2,1,32,4096]{4,3,1,2,0:T(8,128)(2,1)}), bf16[32,2,1,32,4096]{4,3,1,2,0:T(8,128)(2,1)}, u32[]{:S(2)}, u32[]{:S(2)}) async-start(bf16[32,2,1,32,4096]{4,3,1,2,0:T(8,128)(2,1)} %stack.2), calls=%async_computation | async-start | bytes 33554432 | tf_op jit(solution)/shard_map/all_to_all | solution.py:16
  25.1 467.2 %reduce-scatter.2.cloned.1.call-start = ((), (), s32[]{:S(2)}) async-start(), calls=%async_computation.2 | async-start | bytes 2359296 | tf_op jit(solution)/shard_map/reduce_scatter | solution.py:27
Sparse Core Ops, SparseCore 0:
  454.1 38.1 reduce-scatter.1
